TPU v7x, 256 devices: a whole 4x4x8 slice. The times are simulated.
256 devices in a mesh: pipe: 8 (over y, x_lo), dp: 32 (over x_hi, z, core).
Axes of the slice: x: 4 (x_hi: 2, x_lo: 2; x = x_hi * 2 + x_lo), y: 4, z: 8, core: 2. Of those that a mesh axis runs over, the one named last changes fastest.
Arguments:
- acts: bfloat16 [8, 8192, 3072], P('pipe', 'dp'), may hold values from -24 to 24, as said below
- grad: float32 [24576, 4096], P('pipe', 'dp'), may hold values from -6 to 6
- owner_of: int32 [8, 12], replicated, may hold values from 0 to 7, as said below
Outputs:
- precond: float32 [24576, 4096], P('pipe', 'dp')
- held_inverse: float32 [8, 24, 256, 256], P('pipe', None, 'dp')
Inputs may be any that keep to these rules, and one draw needn't show every extreme that they name: `acts`: column and token scales of the activations vary; entries lie within the range. `owner_of`: no section index owns more than 24 blocks in all, and some section index owns exactly 24.
All inputs are finite; a program needn't handle non-finite values.
Results may differ from a plain program's by a relative error of at most 0.0003.
Values sent between devices are 32-bit elements; how exact they have to be, the bound alone decides.
No kernel may reach another device: no remote copies, remote signals or barrier semaphores. Data moves between devices by JAX's collectives and lax.ppermute only.
A program may use at most 64 MiB of HBM per device.

v0:
```python
import jax
import jax.numpy as jnp
from jax import lax
from jax.sharding import Mesh
from jax.sharding import PartitionSpec as P

BLK = 256
HOST = 24
DP = ("dp_0", "dp_1", "dp_2")
damping_ratio = 0.1


def in_blocks(value, dim, count):
    before, after = (value.shape[:dim], value.shape[dim + 1 :])
    return jnp.moveaxis(value.reshape(*before, count, -1, *after), dim, 0)


def summed_on_arrival(value, axis, dim):
    count = lax.axis_size(axis)
    tiles = lax.all_to_all(in_blocks(value, dim, count), axis, 0, 0, tiled=True)
    return jnp.sum(tiles, axis=0)


def from_everyone(value, axis):
    count = lax.axis_size(axis)
    return lax.all_to_all(
        jnp.broadcast_to(value[None], (count, *value.shape)), axis, 0, 0, tiled=True
    )


def in_order(tiles, dim):
    lengths = list(tiles.shape[1:])
    lengths[dim] *= tiles.shape[0]
    return jnp.moveaxis(tiles, 0, dim).reshape(lengths)


def collect(value, axis, dim):
    tiles = from_everyone(value, axis)
    return in_order(tiles, dim)


def turned_blocks(tiles, axes, sequence):
    inside = tiles.shape[1:]
    result = tiles.reshape(*(lax.axis_size(a) for a in axes), *inside)
    for k in sequence:
        result = lax.all_to_all(result, axes[k], k, k, tiled=True)
    return result.reshape(-1, *inside)


def exchange_by_chip(value, groups, sequence, split_dim, concat_dim):
    count = lax.axis_size(groups[0]) * lax.axis_size(groups[1])
    tiles = in_blocks(value, split_dim, count)
    return in_order(turned_blocks(tiles, groups, sequence), concat_dim)


def gather_in_order(value, axes, sequence):
    tiles = value[None]
    for k in sequence:
        tiles = lax.all_gather(tiles, axes[k], axis=0, tiled=True)
    carried = [lax.axis_size(axes[k]) for k in reversed(sequence)]
    tiles = tiles.reshape(*carried, *value.shape)
    turned = sorted(range(len(sequence)), key=lambda place: sequence[len(sequence) - 1 - place])
    return tiles.transpose(*turned, *range(len(sequence), tiles.ndim)).reshape(-1, *value.shape)


def gather_axes(value, axes, sequence, dim):
    return in_order(gather_in_order(value, axes, sequence), dim)


def invert_blocks(factor, vacant):
    order_size = factor.shape[-1]
    diagonal_sum = jnp.sum(jnp.diagonal(factor, axis1=1, axis2=2), axis=1)
    damping = damping_ratio * diagonal_sum / order_size
    identity = jnp.eye(order_size, dtype=factor.dtype)
    shifted = factor + (damping + vacant)[:, None, None] * identity
    cholesky_lower = jnp.linalg.cholesky(shifted)
    identity_stack = jnp.broadcast_to(identity, factor.shape)
    inv_lower = lax.linalg.triangular_solve(
        cholesky_lower, identity_stack, left_side=True, lower=True
    )
    return jnp.einsum("mkr,mkc->mrc", inv_lower, inv_lower, precision=lax.Precision.HIGHEST)


def slot_tables(owner_of):
    owners_flat = owner_of.reshape(-1)
    positions = jnp.arange(owners_flat.shape[0], dtype=jnp.int32)
    matches = owners_flat[:, None] == owners_flat[None, :]
    before = positions[None, :] < positions[:, None]
    slot_rank = jnp.sum((matches & before).astype(jnp.int32), axis=1)
    return (owners_flat, slot_rank)


def shards(acts, grad, owner_of):
    tokens = acts.shape[1]
    feature_count = acts.shape[2]
    nblocks = feature_count // BLK
    data_count = lax.axis_size(DP)
    section_count = lax.axis_size("pipe")
    row_share = BLK // data_count
    all_tokens = tokens * data_count
    section_index = lax.axis_index("pipe")
    member = lax.axis_index(DP)
    features = acts[0].reshape(tokens, nblocks, BLK)
    owners_flat, slot_rank = slot_tables(owner_of)
    slot_ids = jnp.arange(HOST, dtype=jnp.int32)
    pick_mine = (
        (owners_flat[None, :] == section_index) & (slot_rank[None, :] == slot_ids[:, None])
    ).astype(jnp.float32)
    own_owners = lax.dynamic_index_in_dim(owner_of, section_index, 0, keepdims=False)
    own_ranks = lax.dynamic_index_in_dim(
        slot_rank.reshape(section_count, nblocks), section_index, 0, keepdims=False
    )
    target = own_owners * HOST + own_ranks
    pick_back = (
        jnp.arange(section_count * HOST, dtype=jnp.int32)[None, :] == target[:, None]
    ).astype(jnp.float32)
    block_terms = jnp.einsum("tbr,tbc->rbc", features, features, preferred_element_type=jnp.float32)
    my_rows = summed_on_arrival(
        block_terms.reshape(row_share * lax.axis_size(DP), nblocks * BLK), DP, 0
    )
    pieces = collect(my_rows, "pipe", 0).reshape(section_count, row_share, nblocks, BLK)
    hosted = jnp.einsum(
        "jsb,srbc->jrc",
        pick_mine.reshape(HOST, section_count, nblocks),
        pieces,
        precision=lax.Precision.HIGHEST,
    )
    occupied = jnp.sum(pick_mine, axis=1)
    per_member = (HOST + data_count - 1) // data_count
    padded_count = per_member * data_count
    padded = jnp.pad(hosted, ((0, padded_count - HOST), (0, 0), (0, 0)))
    mine_blocks = lax.all_to_all(padded, DP, split_axis=0, concat_axis=1, tiled=True) / all_tokens
    padded_flags = jnp.pad(occupied, (0, padded_count - HOST))
    held_flags = lax.dynamic_slice_in_dim(padded_flags, member * per_member, per_member, 0)
    inverted = invert_blocks(mine_blocks, 1.0 - held_flags) * held_flags[:, None, None]
    spread_rows = exchange_by_chip(inverted, (("dp_0", "dp_1"), "dp_2"), (1, 0), 1, 0)
    held_rows = spread_rows[:HOST]
    returned = collect(held_rows, "pipe", 0)
    own_rows = jnp.einsum("bm,mrc->brc", pick_back, returned, precision=lax.Precision.HIGHEST)
    inverse = gather_axes(own_rows, DP, (0, 1, 2), 1)
    grad_blocks = grad.reshape(nblocks, BLK, grad.shape[1])
    precond = jnp.einsum("brk,bkc->brc", inverse, grad_blocks, precision=lax.Precision.HIGHEST)
    return (precond.reshape(feature_count, grad.shape[1]), held_rows[None])


def solution(mesh):
    torus = Mesh(
        mesh.devices.reshape(mesh.shape["pipe"], 2, 8, 2), ("pipe", "dp_0", "dp_1", "dp_2")
    )
    placed = (P("pipe", DP, None), P("pipe", DP), P())
    return jax.shard_map(
        shards,
        mesh=torus,
        in_specs=placed,
        out_specs=(P("pipe", DP), P("pipe", None, DP, None)),
        check_vma=False,
    )
```

profile of v0, /device:TPU:1, one launch (start us, length us, event | category | flops | bytes accessed | tf_op | source)
XLA Modules:
  0.0 336.6 jit_solution(11809143810914962391)
XLA Ops:
  7.2 0.0 copy-start
  7.2 1.8 copy.50
  9.0 2.3 convolution_bitcast_fusion
  11.3 5.2 %copy.52 = f32[256,12,256]{2,1,0:T(8,128)} copy(f32[256,12,256]{0,2,1:T(8,128)} %convolution_bitcast_fusion) | data formatting | bytes 6291456 | tf_op jit(solution)/shard_map/tbr,tbc->rbc/transpose | solution.py:117
  16.5 4.9 %reshape_reshape.7 = f32[32,8,3072]{2,1,0:T(8,128)} reshape(f32[256,12,256]{2,1,0:T(8,128)} %copy.52) | data formatting | bytes 6291456 | tf_op jit(solution)/shard_map/reshape;reshape | solution.py:15
  21.4 85.4 %all_to_all.34 = f32[32,8,3072]{2,1,0:T(8,128)} all-to-all(f32[32,8,3072]{2,1,0:T(8,128)} %reshape_reshape.7), channel_id=1, replica_groups=mesh['pipe'=8,'dp_0'=2,'dp_1'=8,'dp_2'=2] {'dp_0','dp_1','dp_2'}, dimensions={0} | all-to-all | bytes 6291456 | tf_op jit(solution)/shard_map/all_to_all | solution.py:20
  106.7 2.0 reduce_sum.37
  108.8 0.9 broadcast_in_dim.16
  109.7 4.2 %all-to-all-start.1 = ((f32[8,8,3072]{2,1,0:T(8,128)}), f32[8,8,3072]{2,1,0:T(8,128)S(1)}, u32[]{:S(2)}, u32[]{:S(2)}) async-start(f32[8,8,3072]{2,1,0:T(8,128)} %broadcast_in_dim.16), calls=%async_computation.1 | async-start | bytes 1572864 | tf_op jit(solution)/shard_map/all_to_all | solution.py:26
  114.0 0.1 eq.87
  114.0 0.2 convert_reduce_fusion
  114.2 0.1 reshape.236
  114.3 10.0 %all-to-all-done.1 = f32[8,8,3072]{2,1,0:T(8,128)S(1)} async-done(((f32[8,8,3072]{2,1,0:T(8,128)}), f32[8,8,3072]{2,1,0:T(8,128)S(1)}, u32[]{:S(2)}, u32[]{:S(2)}) %all-to-all-start.1) | async-done | bytes 786464 | tf_op jit(solution)/shard_map/all_to_all | solution.py:26
  124.3 0.7 convolution_bitcast_fusion.1
  125.0 0.1 copy.72
  125.1 0.7 pad.9.clone
  125.8 9.9 %all-to-all-start.2 = ((f32[32,8,256]{2,1,0:T(8,128)}), f32[32,8,256]{2,1,0:T(8,128)S(1)}, u32[]{:S(2)}, u32[]{:S(2)}) async-start(f32[32,8,256]{2,1,0:T(8,128)} %pad.9.clone), calls=%async_computation.2 | async-start | bytes 524288 | tf_op jit(solution)/shard_map/all_to_all | solution.py:132
  135.7 0.1 convert_reduce_fusion.1
  135.9 0.7 fusion.26
  136.6 12.5 %all-to-all-done.2 = f32[32,8,256]{2,1,0:T(8,128)S(1)} async-done(((f32[32,8,256]{2,1,0:T(8,128)}), f32[32,8,256]{2,1,0:T(8,128)S(1)}, u32[]{:S(2)}, u32[]{:S(2)}) %all-to-all-start.2) | async-done | bytes 262176 | tf_op jit(solution)/shard_map/all_to_all | solution.py:132
  149.2 2.3 gather_fusion
  151.5 0.6 reduce.19
  152.1 0.1 copy.55
  153.5 0.1 copy.56
  153.7 11.7 %custom-call.16 = f32[1,128,128]{2,1,0:T(8,128)S(1)} custom-call(f32[1,128,128]{2,1,0:T(8,128)S(1)} %cholesky.114), custom_call_target="Cholesky" | custom-call | tf_op jit(solution)/shard_map/jit(cholesky)/cholesky | solution.py:76
  165.4 9.8 %custom-call.17 = f32[1,1,128,128]{2,3,1,0:T(8,128)S(1)} custom-call(f32[1,1,128,128]{3,2,1,0:T(8,128)S(1)} %get-tuple-element.39), custom_call_target="InvertDiagBlocksLowerTriangular" | custom-call | tf_op jit(solution)/shard_map/jit(cholesky)/cholesky | solution.py:76
  175.3 0.2 fusion.8
  175.5 0.3 fusion.2
  175.7 11.7 %custom-call.18 = f32[1,128,128]{2,1,0:T(8,128)S(1)} custom-call(f32[1,128,128]{2,1,0:T(8,128)S(1)} %fusion.2), custom_call_target="Cholesky" | custom-call | tf_op jit(solution)/shard_map/jit(cholesky)/cholesky | solution.py:76
  187.5 0.1 copy.59
  187.6 0.1 copy.58
  187.7 0.1 copy.57
  187.8 0.6 compare_reduce_fusion
  189.7 0.1 triangular_solve.68
  189.8 4.0 %while.1 = (s32[]{:T(128)}, f32[1,256,256]{1,2,0:T(8,128)S(1)}, s32[2,2]{1,0:T(2,128)S(1)}, f32[2,1,128,128]{3,2,1,0:T(8,128)S(1)}, s32[]{:T(128)}) while((s32[]{:T(128)}, f32[1,256,256]{1,2,0:T(8,128)S(1)}, s32[2,2]{1,0:T(2,128)S(1)}, f32[2,1,128,128]{3,2,1,0:T(8,128)S(1)}, s32[]{:T(128)}) %tuple.31), condition=%wide.while_cond, body=%wide.while_body.sunk | while | flops 2 | bytes 393325 | solution.py:78
  189.8 0.6 fusion.38
  190.4 1.3 constant_dynamic-slice_fusion.7
  191.7 0.1 copy.76
  191.8 0.6 fusion.38
  192.4 1.3 constant_dynamic-slice_fusion.7
  193.7 0.1 copy.76
  193.9 19.9 %custom-call.19 = f32[1,2,128,128]{2,3,1,0:T(8,128)S(1)} custom-call(f32[1,2,128,128]{3,2,1,0:T(8,128)S(1)} %bitcast.115), custom_call_target="InvertDiagBlocksLowerTriangular" | custom-call | tf_op jit(solution)/shard_map/triangular_solve | solution.py:78
  213.8 0.3 fusion.7
  214.0 0.4 fusion.1
  214.4 0.3 convolution_bitcast_fusion.2
  214.8 1.3 convolution_multiply_fusion
  216.1 5.1 %all_to_all.35 = f32[16,2,1,8,256]{4,3,0,2,1:T(8,128)S(1)} all-to-all(f32[16,2,1,8,256]{4,3,0,2,1:T(8,128)S(1)} %copy.62), channel_id=1, replica_groups=mesh['pipe'=8,'dp_0'=2,'dp_1'=8,'dp_2'=2] {'dp_2'}, dimensions={1} | all-to-all | bytes 524288 | tf_op jit(solution)/shard_map/all_to_all | solution.py:46
  221.2 13.1 %all_to_all.36 = f32[16,2,1,8,256]{4,3,1,2,0:T(8,128)S(1)} all-to-all(f32[16,2,1,8,256]{4,3,1,2,0:T(8,128)S(1)} %copy.63), channel_id=1, replica_groups=mesh['pipe'=8,'dp_0'=2,'dp_1'=8,'dp_2'=2] {'dp_0','dp_1'}, dimensions={0} | all-to-all | bytes 524288 | tf_op jit(solution)/shard_map/all_to_all | solution.py:46
  234.3 0.1 copy.64
  234.3 1.3 broadcast_in_dim.20
  235.6 3.6 %all-to-all-start.5 = ((f32[8,24,8,256]{3,1,2,0:T(8,128)}), f32[8,24,8,256]{3,1,2,0:T(8,128)S(1)}, u32[]{:S(2)}, u32[]{:S(2)}) async-start(f32[8,24,8,256]{3,1,2,0:T(8,128)} %broadcast_in_dim.20), calls=%async_computation.5 | async-start | bytes 3145728 | tf_op jit(solution)/shard_map/all_to_all | solution.py:26
  239.2 0.0 all-gather.4.cloned.1.call-start
  239.3 18.9 %all-to-all-done.5 = f32[8,24,8,256]{3,1,2,0:T(8,128)S(1)} async-done(((f32[8,24,8,256]{3,1,2,0:T(8,128)}), f32[8,24,8,256]{3,1,2,0:T(8,128)S(1)}, u32[]{:S(2)}, u32[]{:S(2)}) %all-to-all-start.5) | async-done | bytes 1572896 | tf_op jit(solution)/shard_map/all_to_all | solution.py:26
  258.2 0.1 copy.65
  258.3 0.6 fusion.17
  258.9 0.1 copy.66
  259.0 5.8 %all-gather = f32[24,8,256]{2,1,0:T(8,128)} all-gather(f32[12,8,256]{2,1,0:T(8,128)S(1)} %copy.66), channel_id=2, replica_groups=mesh['pipe'=8,'dp_0'=2,'dp_1'=8,'dp_2'=2] {'dp_0'}, dimensions={0}, use_global_device_ids=true | all-gather | bytes 294912 | tf_op jit(solution)/shard_map/all_gather | solution.py:59
  264.8 0.0 all-gather.4.cloned.1.call-update
  264.8 0.0 all-gather.6.cloned.1.call-start
  264.8 36.0 %all-gather.4.cloned.1.call-done = f32[16,12,8,256]{3,2,1,0:T(8,128)} async-done(((f32[2,12,8,256]{3,2,1,0:T(8,128)}), f32[16,12,8,256]{3,2,1,0:T(8,128)}) %all-gather.4.cloned.1.call-update) | async-done | bytes 1572880 | tf_op jit(solution)/shard_map/all_gather | solution.py:59
  300.9 0.0 all-gather.6.cloned.1.call-update
  300.9 22.4 %all-gather.6.cloned.1.call-done = f32[32,12,8,256]{3,2,1,0:T(8,128)} async-done(((f32[16,12,8,256]{3,2,1,0:T(8,128)}), f32[32,12,8,256]{3,2,1,0:T(8,128)}) %all-gather.6.cloned.1.call-update) | async-done | bytes 3145744 | tf_op jit(solution)/shard_map/all_gather | solution.py:59
  323.3 2.3 copy.67
  325.6 4.1 %fusion.27 = f32[12,256,128]{2,1,0:T(8,128)} fusion(f32[12,256,256]{2,1,0:T(8,128)S(1)} %bitcast.105, f32[12,256,128]{2,1,0:T(8,128)S(1)} %bitcast.102), kind=kOutput, calls=%fused_computation.70 | convolution fusion | flops 1207959552 | bytes 6291456 | tf_op jit(solution)/shard_map/brk,bkc->brc/dot_general | solution.py:142
  (29 shorter events, 0.4 us)
Async XLA Ops:
  7.2 318.5 %copy-start = (f32[3072,128]{1,0:T(8,128)S(1)}, f32[3072,128]{1,0:T(8,128)}, u32[]{:S(2)}) copy-start(f32[3072,128]{1,0:T(8,128)} %param.4) | copy-start | bytes 4718596
  108.8 5.2 %copy-start.2 = (s32[8,12]{1,0:T(8,128)S(1)}, s32[8,12]{1,0:T(8,128)}, u32[]{:S(2)}) copy-start(s32[8,12]{1,0:T(8,128)} %param.5) | copy-start | bytes 1156
  109.7 14.6 %all-to-all-start.1 = ((f32[8,8,3072]{2,1,0:T(8,128)}), f32[8,8,3072]{2,1,0:T(8,128)S(1)}, u32[]{:S(2)}, u32[]{:S(2)}) async-start(f32[8,8,3072]{2,1,0:T(8,128)} %broadcast_in_dim.16), calls=%async_computation.1 | async-start | bytes 1572864 | tf_op jit(solution)/shard_map/all_to_all | solution.py:26
  125.8 23.3 %all-to-all-start.2 = ((f32[32,8,256]{2,1,0:T(8,128)}), f32[32,8,256]{2,1,0:T(8,128)S(1)}, u32[]{:S(2)}, u32[]{:S(2)}) async-start(f32[32,8,256]{2,1,0:T(8,128)} %pad.9.clone), calls=%async_computation.2 | async-start | bytes 524288 | tf_op jit(solution)/shard_map/all_to_all | solution.py:132
  234.2 1.4 copy-start.1
  235.6 22.5 %all-to-all-start.5 = ((f32[8,24,8,256]{3,1,2,0:T(8,128)}), f32[8,24,8,256]{3,1,2,0:T(8,128)S(1)}, u32[]{:S(2)}, u32[]{:S(2)}) async-start(f32[8,24,8,256]{3,1,2,0:T(8,128)} %broadcast_in_dim.20), calls=%async_computation.5 | async-start | bytes 3145728 | tf_op jit(solution)/shard_map/all_to_all | solution.py:26
  239.2 61.7 %all-gather.4.cloned.1.call-start = ((), (), s32[]{:S(2)}) async-start(), calls=%async_computation.6 | async-start | bytes 1769472 | tf_op jit(solution)/shard_map/all_gather | solution.py:59
  264.8 58.6 %all-gather.6.cloned.1.call-start = ((), (), s32[]{:S(2)}) async-start(), calls=%async_computation.7 | async-start | bytes 4718592 | tf_op jit(solution)/shard_map/all_gather | solution.py:59
Sparse Core Ops, SparseCore 0:
  264.9 35.9 all-gather.3
  302.7 20.6 all-gather.5
where the time goes:
time: 337 us
  blocking collectives  109 us (32%)
  waiting for transfers between devices  100 us (30%)
  other arithmetic  57.6 us (17%)
  local copies, waits for them, and re-layouts  24.6 us (7%)
  starting transfers between devices  17.8 us (5%)
  between operations  16.8 us (5%)
  matrix products  10.4 us (3%)
    all_to_all x1, blocking collectives, summed_on_arrival(): tiles = lax.all_to_all(in_blocks(value, dim, count), axis, 0, 0, tiled=True)  85.4 us
    all_gather x2, waiting for transfers between devices, gather_in_order(): tiles = lax.all_gather(tiles, axes[k], axis=0, tiled=True)  58.5 us
    another operation x6, other arithmetic, invert_blocks(): cholesky_lower = jnp.linalg.cholesky(shifted)  33.9 us
    all_to_all x2, waiting for transfers between devices, from_everyone(): lax.all_to_all(jnp.broadcast_to(value[None], (count, *value.shape)), axis...  28.9 us
    another operation x3, other arithmetic, invert_blocks(): lax.linalg.triangular_solve(cholesky_lower, identity_stack, left_side=Tru...  19.9 us
    all_to_all x2, blocking collectives, turned_blocks(): result = lax.all_to_all(result, axes[k], k, k, tiled=True)  18.1 us
    all_to_all x1, waiting for transfers between devices, shards(): lax.all_to_all(padded, DP, split_axis=0, concat_axis=1, tiled=True)  12.5 us
    all_to_all x1, starting transfers between devices, shards(): lax.all_to_all(padded, DP, split_axis=0, concat_axis=1, tiled=True)  9.87 us
  transfers between devices with their start and end apart: 5, of which 5 were waited for; matrix products, arithmetic and copies ran while one was open for 0% of the time, Pallas kernels for 0%

commit v1 on v0

--- a/solution.py
+++ b/solution.py
@@ -56,7 +56,9 @@
 def gather_in_order(value, axes, sequence):
     tiles = value[None]
     for k in sequence:
-        tiles = lax.all_gather(tiles, axes[k], axis=0, tiled=True)
+        tiles = jnp.concatenate(
+            lax.all_to_all(jnp.stack([tiles] * lax.axis_size(axes[k])), axes[k], 0, 0), axis=0
+        )
     carried = [lax.axis_size(axes[k]) for k in reversed(sequence)]
     tiles = tiles.reshape(*carried, *value.shape)
     turned = sorted(range(len(sequence)), key=lambda place: sequence[len(sequence) - 1 - place])

time: 337 us -> 319 us (0.947)
  waiting for transfers between devices: 100 us -> 41.5 us
  blocking collectives: 109 us -> 164 us
  between operations: 16.8 us -> 3.43 us
    all_to_all x0 -> x3, blocking collectives: none -> 60.2 us  [gather_in_order(): lax.all_to_all(jnp.stack([tiles] * lax.axis_size(axes[k])), axes[k], 0, 0)]
    all_gather x2 -> x0, waiting for transfers between devices: 58.5 us -> none  [gather_in_order(): tiles = lax.all_gather(tiles, axes[k], axis=0, tiled=True)]
    all_gather x1 -> x0, blocking collectives: 5.75 us -> none  [gather_in_order(): tiles = lax.all_gather(tiles, axes[k], axis=0, tiled=True)]
  transfers between devices with their start and end apart: 5 -> 3, of which waited for: 5 -> 3; matrix products, arithmetic and copies ran while one was open for 0% -> 0% of each run, Pallas kernels for 0% -> 0%
where the time goes in v1:
time: 319 us; the launch traced here: 318 us
  blocking collectives  164 us (51%)
  other arithmetic  58.1 us (18%)
  waiting for transfers between devices  41.5 us (13%)
  local copies, waits for them, and re-layouts  22.9 us (7%)
  starting transfers between devices  17.7 us (6%)
  matrix products  10.4 us (3%)
  between operations  3.43 us (1%)
    all_to_all x1, blocking collectives, summed_on_arrival(): tiles = lax.all_to_all(in_blocks(value, dim, count), axis, 0, 0, tiled=True)  85.4 us
    all_to_all x3, blocking collectives, gather_in_order(): lax.all_to_all(jnp.stack([tiles] * lax.axis_size(axes[k])), axes[k], 0, 0)  60.2 us
    another operation x6, other arithmetic, invert_blocks(): cholesky_lower = jnp.linalg.cholesky(shifted)  33.9 us
    all_to_all x2, waiting for transfers between devices, from_everyone(): lax.all_to_all(jnp.broadcast_to(value[None], (count, *value.shape)), axis...  28.9 us
    another operation x3, other arithmetic, invert_blocks(): lax.linalg.triangular_solve(cholesky_lower, identity_stack, left_side=Tru...  19.9 us
    all_to_all x2, blocking collectives, turned_blocks(): result = lax.all_to_all(result, axes[k], k, k, tiled=True)  18.1 us
    all_to_all x1, waiting for transfers between devices, shards(): lax.all_to_all(padded, DP, split_axis=0, concat_axis=1, tiled=True)  12.5 us
    all_to_all x1, starting transfers between devices, shards(): lax.all_to_all(padded, DP, split_axis=0, concat_axis=1, tiled=True)  9.87 us
  transfers between devices with their start and end apart: 3, of which 3 were waited for; matrix products, arithmetic and copies ran while one was open for 0% of the time, Pallas kernels for 0%

profile of v1, /device:TPU:1, one launch (start us, length us, event | category | flops | bytes accessed | tf_op | source)
XLA Modules:
  0.0 317.7 jit_solution(10032586673378998228)
XLA Ops:
  0.6 0.0 copy-start
  0.6 1.8 copy.67
  2.5 2.3 convolution_bitcast_fusion
  4.8 5.2 %copy.69 = f32[256,12,256]{2,1,0:T(8,128)} copy(f32[256,12,256]{0,2,1:T(8,128)} %convolution_bitcast_fusion) | data formatting | bytes 6291456 | tf_op jit(solution)/shard_map/tbr,tbc->rbc/transpose | solution.py:119
  10.0 4.9 %reshape_reshape.10 = f32[32,8,3072]{2,1,0:T(8,128)} reshape(f32[256,12,256]{2,1,0:T(8,128)} %copy.69) | data formatting | bytes 6291456 | tf_op jit(solution)/shard_map/reshape;reshape | solution.py:15
  14.8 85.4 %all_to_all.49 = f32[32,8,3072]{2,1,0:T(8,128)} all-to-all(f32[32,8,3072]{2,1,0:T(8,128)} %reshape_reshape.10), channel_id=1, replica_groups=mesh['pipe'=8,'dp_0'=2,'dp_1'=8,'dp_2'=2] {'dp_0','dp_1','dp_2'}, dimensions={0} | all-to-all | bytes 6291456 | tf_op jit(solution)/shard_map/all_to_all | solution.py:20
  100.2 2.0 reduce_sum.37
  102.2 0.0 copy-start.2
  102.3 0.9 broadcast_in_dim.14
  103.2 4.2 %all-to-all-start.1 = ((f32[8,8,3072]{2,1,0:T(8,128)}), f32[8,8,3072]{2,1,0:T(8,128)S(1)}, u32[]{:S(2)}, u32[]{:S(2)}) async-start(f32[8,8,3072]{2,1,0:T(8,128)} %broadcast_in_dim.14), calls=%async_computation.1 | async-start | bytes 1572864 | tf_op jit(solution)/shard_map/all_to_all | solution.py:26
  107.4 0.1 eq.87
  107.5 0.2 convert_reduce_fusion
  107.7 0.1 reshape.235
  107.8 10.0 %all-to-all-done.1 = f32[8,8,3072]{2,1,0:T(8,128)S(1)} async-done(((f32[8,8,3072]{2,1,0:T(8,128)}), f32[8,8,3072]{2,1,0:T(8,128)S(1)}, u32[]{:S(2)}, u32[]{:S(2)}) %all-to-all-start.1) | async-done | bytes 786464 | tf_op jit(solution)/shard_map/all_to_all | solution.py:26
  117.8 0.7 convolution_bitcast_fusion.1
  118.5 0.1 copy.90
  118.6 0.7 pad.9.clone
  119.3 9.9 %all-to-all-start.2 = ((f32[32,8,256]{2,1,0:T(8,128)}), f32[32,8,256]{2,1,0:T(8,128)S(1)}, u32[]{:S(2)}, u32[]{:S(2)}) async-start(f32[32,8,256]{2,1,0:T(8,128)} %pad.9.clone), calls=%async_computation.2 | async-start | bytes 524288 | tf_op jit(solution)/shard_map/all_to_all | solution.py:134
  129.2 0.1 convert_reduce_fusion.1
  129.3 0.7 fusion.28
  130.0 12.5 %all-to-all-done.2 = f32[32,8,256]{2,1,0:T(8,128)S(1)} async-done(((f32[32,8,256]{2,1,0:T(8,128)}), f32[32,8,256]{2,1,0:T(8,128)S(1)}, u32[]{:S(2)}, u32[]{:S(2)}) %all-to-all-start.2) | async-done | bytes 262176 | tf_op jit(solution)/shard_map/all_to_all | solution.py:134
  142.6 2.3 gather_fusion
  145.0 0.6 reduce.19
  145.6 0.1 copy.72
  147.0 0.1 copy.73
  147.2 11.7 %custom-call.16 = f32[1,128,128]{2,1,0:T(8,128)S(1)} custom-call(f32[1,128,128]{2,1,0:T(8,128)S(1)} %cholesky.114), custom_call_target="Cholesky" | custom-call | tf_op jit(solution)/shard_map/jit(cholesky)/cholesky | solution.py:78
  158.9 9.8 %custom-call.17 = f32[1,1,128,128]{2,3,1,0:T(8,128)S(1)} custom-call(f32[1,1,128,128]{3,2,1,0:T(8,128)S(1)} %get-tuple-element.43), custom_call_target="InvertDiagBlocksLowerTriangular" | custom-call | tf_op jit(solution)/shard_map/jit(cholesky)/cholesky | solution.py:78
  168.7 0.2 fusion.11
  168.9 0.3 fusion.5
  169.2 11.7 %custom-call.18 = f32[1,128,128]{2,1,0:T(8,128)S(1)} custom-call(f32[1,128,128]{2,1,0:T(8,128)S(1)} %fusion.5), custom_call_target="Cholesky" | custom-call | tf_op jit(solution)/shard_map/jit(cholesky)/cholesky | solution.py:78
  181.0 0.1 copy.76
  181.1 0.1 copy.75
  181.2 0.1 copy.74
  181.3 0.6 compare_reduce_fusion
  183.2 0.1 triangular_solve.68
  183.3 4.0 %while.1 = (s32[]{:T(128)}, f32[1,256,256]{1,2,0:T(8,128)S(1)}, s32[2,2]{1,0:T(2,128)S(1)}, f32[2,1,128,128]{3,2,1,0:T(8,128)S(1)}, s32[]{:T(128)}) while((s32[]{:T(128)}, f32[1,256,256]{1,2,0:T(8,128)S(1)}, s32[2,2]{1,0:T(2,128)S(1)}, f32[2,1,128,128]{3,2,1,0:T(8,128)S(1)}, s32[]{:T(128)}) %tuple.32), condition=%wide.while_cond, body=%wide.while_body.sunk | while | flops 2 | bytes 393325 | solution.py:80
  183.3 0.6 fusion.38
  183.9 1.3 constant_dynamic-slice_fusion.7
  185.2 0.1 copy.98
  185.3 0.6 fusion.38
  185.9 1.3 constant_dynamic-slice_fusion.7
  187.2 0.1 copy.98
  187.3 19.9 %custom-call.19 = f32[1,2,128,128]{2,3,1,0:T(8,128)S(1)} custom-call(f32[1,2,128,128]{3,2,1,0:T(8,128)S(1)} %bitcast.119), custom_call_target="InvertDiagBlocksLowerTriangular" | custom-call | tf_op jit(solution)/shard_map/triangular_solve | solution.py:80
  207.2 0.3 fusion.10
  207.5 0.4 fusion.4
  207.9 0.3 convolution_bitcast_fusion.2
  208.2 1.3 convolution_multiply_fusion
  209.5 5.1 %all_to_all.50 = f32[16,2,1,8,256]{4,3,0,2,1:T(8,128)S(1)} all-to-all(f32[16,2,1,8,256]{4,3,0,2,1:T(8,128)S(1)} %copy.79), channel_id=1, replica_groups=mesh['pipe'=8,'dp_0'=2,'dp_1'=8,'dp_2'=2] {'dp_2'}, dimensions={1} | all-to-all | bytes 524288 | tf_op jit(solution)/shard_map/all_to_all | solution.py:46
  214.6 13.1 %all_to_all.51 = f32[16,2,1,8,256]{4,3,1,2,0:T(8,128)S(1)} all-to-all(f32[16,2,1,8,256]{4,3,1,2,0:T(8,128)S(1)} %copy.80), channel_id=1, replica_groups=mesh['pipe'=8,'dp_0'=2,'dp_1'=8,'dp_2'=2] {'dp_0','dp_1'}, dimensions={0} | all-to-all | bytes 524288 | tf_op jit(solution)/shard_map/all_to_all | solution.py:46
  227.7 0.0 copy-start.1
  227.7 0.1 copy.81
  227.8 1.3 broadcast_in_dim.16
  229.1 3.6 %all-to-all-start.5 = ((f32[8,24,8,256]{3,1,2,0:T(8,128)}), f32[8,24,8,256]{3,1,2,0:T(8,128)S(1)}, u32[]{:S(2)}, u32[]{:S(2)}) async-start(f32[8,24,8,256]{3,1,2,0:T(8,128)} %broadcast_in_dim.16), calls=%async_computation.5 | async-start | bytes 3145728 | tf_op jit(solution)/shard_map/all_to_all | solution.py:26
  232.7 18.9 %all-to-all-done.5 = f32[8,24,8,256]{3,1,2,0:T(8,128)S(1)} async-done(((f32[8,24,8,256]{3,1,2,0:T(8,128)}), f32[8,24,8,256]{3,1,2,0:T(8,128)S(1)}, u32[]{:S(2)}, u32[]{:S(2)}) %all-to-all-start.5) | async-done | bytes 1572896 | tf_op jit(solution)/shard_map/all_to_all | solution.py:26
  251.6 0.1 copy.82
  251.8 0.6 convolution_bitcast_fusion.4
  252.4 0.1 copy.83
  252.6 7.6 %all_to_all.52 = f32[2,1,12,8,256]{4,3,2,1,0:T(8,128)S(1)} all-to-all(f32[2,1,12,8,256]{4,3,2,1,0:T(8,128)S(1)} %copy.83), channel_id=1, replica_groups=mesh['pipe'=8,'dp_0'=2,'dp_1'=8,'dp_2'=2] {'dp_0'}, dimensions={0} | all-to-all | bytes 393216 | tf_op jit(solution)/shard_map/all_to_all | solution.py:60
  260.1 0.1 stack.10
  260.3 41.3 %all_to_all.53 = f32[8,2,12,8,256]{4,3,2,1,0:T(8,128)S(1)} all-to-all(f32[8,2,12,8,256]{4,3,2,1,0:T(8,128)S(1)} %stack.10), channel_id=1, replica_groups=mesh['pipe'=8,'dp_0'=2,'dp_1'=8,'dp_2'=2] {'dp_1'}, dimensions={0} | all-to-all | bytes 3145728 | tf_op jit(solution)/shard_map/all_to_all | solution.py:60
  301.6 0.4 pad_maximum_fusion
  302.0 11.3 %all_to_all.54 = f32[2,16,12,8,256]{4,3,2,1,0:T(8,128)S(1)} all-to-all(f32[2,16,12,8,256]{4,3,2,1,0:T(8,128)S(1)} %pad_maximum_fusion), channel_id=1, replica_groups=mesh['pipe'=8,'dp_0'=2,'dp_1'=8,'dp_2'=2] {'dp_2'}, dimensions={0} | all-to-all | bytes 6291456 | tf_op jit(solution)/shard_map/all_to_all | solution.py:60
  313.3 0.3 copy.84
  313.6 4.1 %fusion = f32[12,256,128]{2,1,0:T(8,128)} fusion(f32[12,256,128]{2,1,0:T(8,128)S(1)} %bitcast.105, f32[12,32,8,256]{3,2,0,1:T(8,128)S(1)} %bitcast.109), kind=kOutput, calls=%fused_computation.5 | convolution fusion | flops 1207959552 | bytes 6291456 | tf_op jit(solution)/shard_map/brk,bkc->brc/dot_general | solution.py:144
  (28 shorter events, 0.4 us)
Async XLA Ops:
  0.6 313.0 %copy-start = (f32[3072,128]{1,0:T(8,128)S(1)}, f32[3072,128]{1,0:T(8,128)}, u32[]{:S(2)}) copy-start(f32[3072,128]{1,0:T(8,128)} %param.4) | copy-start | bytes 4718596
  102.2 5.2 %copy-start.2 = (s32[8,12]{1,0:T(8,128)S(1)}, s32[8,12]{1,0:T(8,128)}, u32[]{:S(2)}) copy-start(s32[8,12]{1,0:T(8,128)} %param.5) | copy-start | bytes 1156
  103.2 14.6 %all-to-all-start.1 = ((f32[8,8,3072]{2,1,0:T(8,128)}), f32[8,8,3072]{2,1,0:T(8,128)S(1)}, u32[]{:S(2)}, u32[]{:S(2)}) async-start(f32[8,8,3072]{2,1,0:T(8,128)} %broadcast_in_dim.14), calls=%async_computation.1 | async-start | bytes 1572864 | tf_op jit(solution)/shard_map/all_to_all | solution.py:26
  119.3 23.3 %all-to-all-start.2 = ((f32[32,8,256]{2,1,0:T(8,128)}), f32[32,8,256]{2,1,0:T(8,128)S(1)}, u32[]{:S(2)}, u32[]{:S(2)}) async-start(f32[32,8,256]{2,1,0:T(8,128)} %pad.9.clone), calls=%async_computation.2 | async-start | bytes 524288 | tf_op jit(solution)/shard_map/all_to_all | solution.py:134
  227.7 1.4 copy-start.1
  229.1 22.5 %all-to-all-start.5 = ((f32[8,24,8,256]{3,1,2,0:T(8,128)}), f32[8,24,8,256]{3,1,2,0:T(8,128)S(1)}, u32[]{:S(2)}, u32[]{:S(2)}) async-start(f32[8,24,8,256]{3,1,2,0:T(8,128)} %broadcast_in_dim.16), calls=%async_computation.5 | async-start | bytes 3145728 | tf_op jit(solution)/shard_map/all_to_all | solution.py:26
